TPU v7x, 32 devices: a whole 2x2x4 slice. The times are simulated.
32 devices in a mesh: dp: 16 (over z, y, core), tensor: 2 (over x).
Axes of the slice: x: 2, y: 2, z: 4, core: 2. Of those that a mesh axis runs over, the one named last changes fastest.
Arguments:
- tokens: bfloat16 [16384, 768], P(('dp', 'tensor')), may hold values from -6 to 6
- query_weight: bfloat16 [768, 768], P('dp', 'tensor'), may hold values from -0.21875 to 0.21875
- query_bias: float32 [768], replicated, may hold values from -3 to 3
- key_weight: bfloat16 [768, 768], P('dp', 'tensor'), may hold values from -0.21875 to 0.21875
- value_weight: bfloat16 [768, 768], P('dp', 'tensor'), may hold values from -0.21875 to 0.21875
- value_bias: float32 [768], replicated, may hold values from -0.625 to 0.625
- output_weight: bfloat16 [768, 768], P('tensor', 'dp'), may hold values from -1.25 to 1.25
- output_bias: float32 [768], replicated, may hold values from -3 to 3
- first_gain: float32 [768], replicated, may hold values from 0.5 to 1.5
- first_shift: float32 [768], replicated, may hold values from -3 to 3
- inner_weight: bfloat16 [768, 3072], P('dp', 'tensor'), may hold values from -0.21875 to 0.21875
- inner_bias: float32 [3072], replicated, may hold values from -3 to 3
- outer_weight: bfloat16 [3072, 768], P('tensor', 'dp'), may hold values from -0.109375 to 0.109375
- outer_bias: float32 [768], replicated, may hold values from -3 to 3
- second_gain: float32 [768], replicated, may hold values from 0.5 to 1.5
- second_shift: float32 [768], replicated, may hold values from -3 to 3
- segments: int32 [16, 1024], P('dp'), may hold values from 0 to 7, never falling along the last dimension, each value on 1 to 768 neighbouring positions
- valid_length: int32 [16], P('dp'), may hold values from 512 to 1024
- cotangent: bfloat16 [16384, 768], P(('dp', 'tensor')), may hold values from -6 to 6
Outputs:
- layer_output: bfloat16 [16384, 768], P(('dp', 'tensor'))
- input_gradient: float32 [16384, 768], P(('dp', 'tensor'))
- query_weight_gradient: float32 [768, 768], P('dp', 'tensor')
- query_bias_gradient: float32 [768], replicated
- key_weight_gradient: float32 [768, 768], P('dp', 'tensor')
- value_weight_gradient: float32 [768, 768], P('dp', 'tensor')
- value_bias_gradient: float32 [768], replicated
- output_weight_gradient: float32 [768, 768], P('tensor', 'dp')
- output_bias_gradient: float32 [768], replicated
- first_gain_gradient: float32 [768], replicated
- first_shift_gradient: float32 [768], replicated
- inner_weight_gradient: float32 [768, 3072], P('dp', 'tensor')
- inner_bias_gradient: float32 [3072], replicated
- outer_weight_gradient: float32 [3072, 768], P('tensor', 'dp')
- outer_bias_gradient: float32 [768], replicated
- second_gain_gradient: float32 [768], replicated
- second_shift_gradient: float32 [768], replicated
Inputs may be any that keep to these rules, and one draw needn't show every extreme that they name: `segments`: segment numbers never fall along a sequence; a token attends only to tokens of its own document. tokens of a sequence at positions valid_length and beyond are padding: no query attends to them as keys except the token itself.
All inputs are finite; a program needn't handle non-finite values.
Results may differ from a plain program's by a relative error of at most 0.013.
Values may be sent and summed in bfloat16 or wider, within the bound.
No kernel may reach another device: no remote copies, remote signals or barrier semaphores. Data moves between devices by JAX's collectives and lax.ppermute only.
A program may use at most 128 MiB of HBM per device.

v0:
```python
import jax
import jax.numpy as jnp
from jax import lax
from jax.sharding import PartitionSpec as P

HEAD_DIM = 64
norm_epsilon = 1e-12
masked_score = -1e30


def normalize(matrix, gain, shift):
    center = matrix - jnp.mean(matrix, axis=-1, keepdims=True)
    spread = jnp.mean(center * center, axis=-1, keepdims=True)
    return center * lax.rsqrt(spread + norm_epsilon) * gain + shift


def block_scores(query_block, key_seq, segment_row, valid_count, first_row):
    block_rows = query_block.shape[0]
    length = key_seq.shape[0]
    scores = (
        jnp.einsum("qhd,khd->hqk", query_block, key_seq, preferred_element_type=jnp.float32) * 0.125
    )
    positions = jnp.arange(length, dtype=jnp.int32)
    query_pos = first_row + jnp.arange(block_rows, dtype=jnp.int32)
    query_seg = lax.dynamic_slice_in_dim(segment_row, first_row, block_rows)
    allowed = (query_seg[:, None] == segment_row[None, :]) & (
        (positions[None, :] < valid_count) | (query_pos[:, None] == positions[None, :])
    )
    return jnp.where(allowed[None], scores, masked_score)


def attend_sequence(pieces):
    query_seq, key_seq, value_seq, segment_row, valid_count = pieces
    length = query_seq.shape[0]
    block_rows = min(512, length)

    def one_block(block_index):
        first_row = block_index * block_rows
        query_block = lax.dynamic_slice_in_dim(query_seq, first_row, block_rows)
        masked = block_scores(query_block, key_seq, segment_row, valid_count, first_row)
        largest = jnp.max(masked, axis=-1, keepdims=True)
        totals = jnp.sum(jnp.exp(masked - largest), axis=-1, keepdims=True)
        log_total = largest + jnp.log(totals)
        probs_low = jnp.exp(masked - log_total).astype(jnp.bfloat16)
        context = jnp.einsum(
            "hqk,khd->qhd", probs_low, value_seq, preferred_element_type=jnp.float32
        )
        return (context.astype(jnp.bfloat16), log_total[..., 0])

    contexts, log_totals = lax.map(one_block, jnp.arange(length // block_rows, dtype=jnp.int32))
    return (contexts.reshape(query_seq.shape), log_totals)


def attend_backward(pieces):
    query_seq, key_seq, value_seq, segment_row, valid_count, grad_seq, log_totals = pieces
    length = query_seq.shape[0]
    block_rows = min(512, length)

    def one_block(running, inputs):
        key_grad, value_grad = running
        block_index, log_total = inputs
        first_row = block_index * block_rows
        query_block = lax.dynamic_slice_in_dim(query_seq, first_row, block_rows)
        grad_block = lax.dynamic_slice_in_dim(grad_seq, first_row, block_rows)
        masked = block_scores(query_block, key_seq, segment_row, valid_count, first_row)
        probs = jnp.exp(masked - log_total[..., None])
        probs_low = probs.astype(jnp.bfloat16)
        value_grad = value_grad + jnp.einsum(
            "hqk,qhd->khd", probs_low, grad_block, preferred_element_type=jnp.float32
        )
        d_probs = jnp.einsum(
            "qhd,khd->hqk", grad_block, value_seq, preferred_element_type=jnp.float32
        )
        row_inner = jnp.sum(probs * d_probs, axis=-1, keepdims=True)
        d_scores = (probs * (d_probs - row_inner)).astype(jnp.bfloat16)
        query_grad = (
            jnp.einsum("hqk,khd->qhd", d_scores, key_seq, preferred_element_type=jnp.float32)
            * 0.125
        )
        key_grad = (
            key_grad
            + jnp.einsum("hqk,qhd->khd", d_scores, query_block, preferred_element_type=jnp.float32)
            * 0.125
        )
        return ((key_grad, value_grad), query_grad.astype(jnp.bfloat16))

    empty = jnp.zeros(key_seq.shape, jnp.float32)
    block_ids = jnp.arange(length // block_rows, dtype=jnp.int32)
    (key_grad, value_grad), query_grads = lax.scan(
        one_block, (empty, empty), (block_ids, log_totals)
    )
    return (
        query_grads.reshape(query_seq.shape),
        key_grad.astype(jnp.bfloat16),
        value_grad.astype(jnp.bfloat16),
    )


def slope_and_gelu(inner):
    rise = 0.5 * (1.0 + lax.erf(inner * 0.7071067811865476))
    density = jnp.exp(-0.5 * inner * inner) * 0.3989422804014327
    return (inner * rise, rise + inner * density)


def norm_backward(matrix, gain, grad):
    center = matrix - jnp.mean(matrix, axis=-1, keepdims=True)
    spread = jnp.mean(center * center, axis=-1, keepdims=True)
    scale = lax.rsqrt(spread + norm_epsilon)
    normed = center * scale
    d_normed = grad * gain
    pulled = scale * (
        d_normed
        - jnp.mean(d_normed, axis=-1, keepdims=True)
        - normed * jnp.mean(d_normed * normed, axis=-1, keepdims=True)
    )
    return (pulled, jnp.sum(grad * normed, axis=0), jnp.sum(grad, axis=0))


def halves_in_order(mine, other, shard_index):
    first = shard_index == 0
    return (jnp.where(first, mine, other), jnp.where(first, other, mine))


def mix(left, right, dims):
    return lax.dot_general(left, right, (dims, ((), ())), preferred_element_type=jnp.float32)


def on_device(
    tokens,
    query_weight,
    query_bias,
    key_weight,
    value_weight,
    value_bias,
    output_weight,
    output_bias,
    first_gain,
    first_shift,
    inner_weight,
    inner_bias,
    outer_weight,
    outer_bias,
    second_gain,
    second_shift,
    segments,
    valid_length,
    cotangent,
):
    low = jnp.bfloat16
    whole = ("tensor", "dp")
    swap = [(0, 1), (1, 0)]
    own_rows, width = tokens.shape
    head_cols = query_weight.shape[1]
    hidden_cols = inner_weight.shape[1]
    local_heads = head_cols // HEAD_DIM
    shard_index = lax.axis_index("tensor")
    own_start = shard_index * own_rows
    other_start = (1 - shard_index) * own_rows
    other_tokens = lax.ppermute(tokens, "tensor", swap)
    full_qkv = lax.all_gather(
        jnp.concatenate([query_weight, key_weight, value_weight], axis=1), "dp", axis=0, tiled=True
    )
    full_output = lax.all_gather(output_weight.T, whole, axis=0, tiled=True)
    full_inner = lax.all_gather(inner_weight, whole, axis=0, tiled=True)
    full_outer = lax.all_gather(outer_weight.T, whole, axis=0, tiled=True)
    full_output = full_output.reshape(2, width, head_cols)
    full_inner = full_inner.reshape(2, width, hidden_cols)
    full_outer = full_outer.reshape(2, width, hidden_cols)
    group_rows = jnp.concatenate(halves_in_order(tokens, other_tokens, shard_index), axis=0)
    bias_query = lax.dynamic_slice_in_dim(query_bias, shard_index * head_cols, head_cols)
    bias_value = lax.dynamic_slice_in_dim(value_bias, shard_index * head_cols, head_cols)
    bias_qkv = jnp.concatenate([bias_query, jnp.zeros_like(bias_query), bias_value])
    seq_count, seq_length = segments.shape
    four_shape = (seq_count, seq_length, local_heads, HEAD_DIM)
    qkv = (mix(group_rows, full_qkv, ((1,), (0,))) + bias_qkv).astype(low)
    queries = qkv[:, :head_cols].reshape(four_shape)
    keys_all = qkv[:, head_cols : 2 * head_cols].reshape(four_shape)
    values_all = qkv[:, 2 * head_cols :].reshape(four_shape)
    contexts, log_totals = lax.map(
        attend_sequence, (queries, keys_all, values_all, segments, valid_length)
    )
    context = contexts.reshape(seq_count * seq_length, head_cols)
    own_context = lax.dynamic_slice_in_dim(context, own_start, own_rows)
    far_context = lax.ppermute(
        lax.dynamic_slice_in_dim(context, other_start, own_rows), "tensor", swap
    )
    context_halves = halves_in_order(own_context, far_context, shard_index)
    attended = mix(context_halves[0], full_output[0], ((1,), (1,))) + mix(
        context_halves[1], full_output[1], ((1,), (1,))
    )
    first_sum = tokens.astype(jnp.float32) + attended + output_bias
    hidden = normalize(first_sum, first_gain, first_shift)
    hidden_low = hidden.astype(low)
    activated, slopes = ([], [])
    outer = outer_bias
    for half in range(2):
        inner = (
            mix(hidden_low, full_inner[half], ((1,), (0,)))
            + inner_bias[half * hidden_cols : (half + 1) * hidden_cols]
        )
        value, slope = slope_and_gelu(inner)
        activated.append(value.astype(low))
        slopes.append(slope)
        outer = outer + mix(activated[half], full_outer[half], ((1,), (1,)))
    second_sum = hidden + outer
    layer_output = normalize(second_sum, second_gain, second_shift).astype(low)
    d_second, second_gain_grad, second_shift_grad = norm_backward(
        second_sum, second_gain, cotangent.astype(jnp.float32)
    )
    outer_bias_grad = jnp.sum(d_second, axis=0)
    d_outer = d_second.astype(low)
    outer_weight_grad = jnp.stack(
        [mix(d_outer, activated[half], ((0,), (0,))).astype(low) for half in range(2)]
    )
    d_hidden = d_second
    inner_grads, inner_bias_parts = ([], [])
    for half in range(2):
        d_activated = mix(d_outer, full_outer[half], ((1,), (0,)))
        d_inner = (d_activated * slopes[half]).astype(low)
        inner_grads.append(mix(hidden_low, d_inner, ((0,), (0,))).astype(low))
        inner_bias_parts.append(jnp.sum(d_inner, axis=0, dtype=jnp.float32))
        d_hidden = d_hidden + mix(d_inner, full_inner[half], ((1,), (1,)))
    inner_weight_grad = jnp.stack(inner_grads)
    inner_bias_grad = jnp.concatenate(inner_bias_parts)
    d_first, first_gain_grad, first_shift_grad = norm_backward(first_sum, first_gain, d_hidden)
    output_bias_grad = jnp.sum(d_first, axis=0)
    d_attended = d_first.astype(low)
    output_weight_grad = jnp.stack(
        [mix(d_attended, context_halves[half], ((0,), (0,))).astype(low) for half in range(2)]
    )
    d_context_halves = [
        mix(d_attended, full_output[half], ((1,), (0,))).astype(low) for half in range(2)
    ]
    first = shard_index == 0
    own_d_context = jnp.where(first, d_context_halves[0], d_context_halves[1])
    far_d_context = lax.ppermute(
        jnp.where(first, d_context_halves[1], d_context_halves[0]), "tensor", swap
    )
    d_context = jnp.concatenate(halves_in_order(own_d_context, far_d_context, shard_index), axis=0)
    d_queries, d_keys, d_values = lax.map(
        attend_backward,
        (
            queries,
            keys_all,
            values_all,
            segments,
            valid_length,
            d_context.reshape(four_shape),
            log_totals,
        ),
    )
    flat = (seq_count * seq_length, head_cols)
    d_qkv = jnp.concatenate(
        [d_queries.reshape(flat), d_keys.reshape(flat), d_values.reshape(flat)], axis=1
    )
    qkv_weight_grad = mix(group_rows, d_qkv, ((0,), (0,))).astype(low)
    partial_input = mix(d_qkv, full_qkv, ((1,), (1,)))
    far_input = lax.ppermute(
        lax.dynamic_slice_in_dim(partial_input, other_start, own_rows).astype(low), "tensor", swap
    )
    input_gradient = (
        d_first
        + lax.dynamic_slice_in_dim(partial_input, own_start, own_rows)
        + far_input.astype(jnp.float32)
    )

    def scatter(partial, axes):
        return lax.psum_scatter(
            partial.reshape(-1, partial.shape[-1]), axes, scatter_dimension=0, tiled=True
        ).astype(jnp.float32)

    outer_shard = scatter(outer_weight_grad, whole).T
    inner_shard = scatter(inner_weight_grad, whole)
    output_shard = scatter(output_weight_grad, whole).T
    qkv_shard = scatter(qkv_weight_grad, ("dp",))
    bias_local = jnp.sum(d_qkv, axis=0, dtype=jnp.float32)
    spread_out = lax.dynamic_update_slice(
        jnp.zeros((2, width), jnp.float32),
        jnp.stack([bias_local[:head_cols], bias_local[2 * head_cols :]]),
        (0, shard_index * head_cols),
    )
    pieces = [
        spread_out.reshape(-1),
        output_bias_grad,
        first_gain_grad,
        first_shift_grad,
        outer_bias_grad,
        second_gain_grad,
        second_shift_grad,
        inner_bias_grad,
    ]
    summed = lax.psum(jnp.concatenate(pieces), ("dp", "tensor"))
    rows = summed[: 8 * width].reshape(8, width)
    return (
        layer_output,
        input_gradient,
        qkv_shard[:, :head_cols],
        rows[0],
        qkv_shard[:, head_cols : 2 * head_cols],
        qkv_shard[:, 2 * head_cols :],
        rows[1],
        output_shard,
        rows[2],
        rows[3],
        rows[4],
        inner_shard,
        summed[8 * width :],
        outer_shard,
        rows[5],
        rows[6],
        rows[7],
    )


def solution(mesh):
    placed = (
        P(("dp", "tensor"), None),
        P("dp", "tensor"),
        P(),
        P("dp", "tensor"),
        P("dp", "tensor"),
        P(),
        P("tensor", "dp"),
        P(),
        P(),
        P(),
        P("dp", "tensor"),
        P(),
        P("tensor", "dp"),
        P(),
        P(),
        P(),
        P("dp", None),
        P("dp"),
        P(("dp", "tensor"), None),
    )
    return jax.shard_map(
        on_device,
        mesh=mesh,
        in_specs=placed,
        out_specs=(
            P(("dp", "tensor"), None),
            P(("dp", "tensor"), None),
            P("dp", "tensor"),
            P(),
            P("dp", "tensor"),
            P("dp", "tensor"),
            P(),
            P("tensor", "dp"),
            P(),
            P(),
            P(),
            P("dp", "tensor"),
            P(),
            P("tensor", "dp"),
            P(),
            P(),
            P(),
        ),
        check_vma=False,
    )
```

profile of v0, /device:TPU:0, one launch (start us, length us, event | category | flops | bytes accessed | tf_op | source)
XLA Modules:
  0.0 660.5 jit_solution(15233943400228055662)
XLA Ops:
  7.2 1.5 pad_maximum_fusion.8
  10.3 3.0 collective-permute-start
  14.9 16.1 %collective-permute-done = bf16[512,768]{1,0:T(8,128)(2,1)S(1)} collective-permute-done((bf16[512,768]{1,0:T(8,128)(2,1)}, bf16[512,768]{1,0:T(8,128)(2,1)S(1)}, u32[]{:S(2)}, u32[]{:S(2)}) %collective-permute-start) | collective-permute-done | bytes 786464 | tf_op jit(solution)/shard_map/ppermute | solution.py:159
  32.3 21.4 %all-gather.5.cloned.1.call-done = bf16[768,1152]{1,0:T(8,128)(2,1)} async-done(((bf16[48,1152]{1,0:T(8,128)(2,1)}), bf16[768,1152]{1,0:T(8,128)(2,1)}) %all-gather.5.cloned.1.call-update) | async-done | bytes 1769488 | tf_op jit(solution)/shard_map/all_gather | solution.py:160
  53.7 3.7 add_convert_fusion
  58.6 35.0 %while.47 = (s32[]{:T(128)}, bf16[2,512,6,64]{1,3,2,0:T(8,128)(2,1)S(1)}, f32[2,6,512]{2,1,0:T(8,128)S(1)}, s32[2]{0:T(128)S(1)}, s32[1024]{0:T(1024)S(1)}, /*in...) while((s32[]{:T(128)}, ...), condition=%wide.region_3.4_spmd, body=%wide.region_0.3_spmd.sunk | while | flops 842201600 | bytes 92672224 | solution.py:50
  61.4 2.4 fusion.143
  63.9 3.7 exponential_reduce_fusion.2
  68.4 7.8 %fusion.144 = bf16[2,512,6,64]{1,3,2,0:T(8,128)(2,1)S(1)} fusion(bf16[2,512,6,64]{1,3,2,0:T(8,128)(2,1)S(1)} %get-tuple-element.507, s32[]{:T(128)} %get-tuple-element.506, bf16[1024,6,64]{0,2,1:T(8,128)(2,1)S(1)} %get-tuple-element.527, f32[6,512,1024]{2,1,0:T(8,128)} %copy-done.2, f32[6,512]{1,0:T(8,128)S(1)} %get-tuple-element.477, ...), kind=kOutput, calls=%fused_computation.11.clone.1 | convolution fusion | flops 415432704 | bytes 14303236 | tf_op jit(solution)/shard_map/while/body/eval_jaxpr/while/body/eval_jaxpr/hqk,khd->qhd/dot_general | solution.py:45
  78.8 2.4 fusion.143
  81.3 3.7 exponential_reduce_fusion.2
  85.8 7.8 %fusion.144 = bf16[2,512,6,64]{1,3,2,0:T(8,128)(2,1)S(1)} fusion(bf16[2,512,6,64]{1,3,2,0:T(8,128)(2,1)S(1)} %get-tuple-element.507, s32[]{:T(128)} %get-tuple-element.506, bf16[1024,6,64]{0,2,1:T(8,128)(2,1)S(1)} %get-tuple-element.527, f32[6,512,1024]{2,1,0:T(8,128)} %copy-done.2, f32[6,512]{1,0:T(8,128)S(1)} %get-tuple-element.477, ...), kind=kOutput, calls=%fused_computation.11.clone.1 | convolution fusion | flops 415432704 | bytes 14303236 | tf_op jit(solution)/shard_map/while/body/eval_jaxpr/while/body/eval_jaxpr/hqk,khd->qhd/dot_general | solution.py:45
  95.5 1.9 copy.53
  97.4 1.6 collective-permute-start.1
  100.2 9.4 %all-gather.7.cloned.1.call-done = bf16[1536,384]{1,0:T(8,128)(2,1)} async-done(((bf16[48,384]{1,0:T(8,128)(2,1)}), bf16[1536,384]{1,0:T(8,128)(2,1)}) %all-gather.7.cloned.1.call-update) | async-done | bytes 1179664 | tf_op jit(solution)/shard_map/all_gather | solution.py:163
  109.7 1.8 fusion.77
  111.5 1.9 fusion.92
  115.8 60.4 %all-gather.9.cloned.1.call-done = bf16[1536,1536]{1,0:T(8,128)(2,1)} async-done(((bf16[48,1536]{1,0:T(8,128)(2,1)}), bf16[1536,1536]{1,0:T(8,128)(2,1)}) %all-gather.9.cloned.1.call-update) | async-done | bytes 4718608 | tf_op jit(solution)/shard_map/all_gather | solution.py:164
  176.2 5.8 multiply_convert_fusion.1
  182.0 3.5 multiply_convert_fusion.2
  185.5 55.4 %all-gather.11.cloned.1.call-done = bf16[1536,1536]{1,0:T(8,128)(2,1)} async-done(((bf16[48,1536]{1,0:T(8,128)(2,1)}), bf16[1536,1536]{1,0:T(8,128)(2,1)}) %all-gather.11.cloned.1.call-update) | async-done | bytes 4718608 | tf_op jit(solution)/shard_map/all_gather | solution.py:165
  240.9 3.7 fusion.54
  245.4 1.7 fusion.93
  248.7 2.1 fusion.84
  250.9 3.2 convert_reduce_fusion.2
  254.1 3.2 convert_reduce_fusion.1
  257.3 1.4 fusion.56
  258.7 2.3 multiply_reduce_fusion.1
  262.2 1.8 copy-done.14
  264.6 1.5 broadcast_select_fusion.4
  266.0 1.4 collective-permute-start.2
  269.9 7.7 %collective-permute-done.2 = bf16[512,384]{1,0:T(8,128)(2,1)} collective-permute-done((bf16[512,384]{1,0:T(8,128)(2,1)}, bf16[512,384]{1,0:T(8,128)(2,1)}, u32[]{:S(2)}, u32[]{:S(2)}) %collective-permute-start.2) | collective-permute-done | bytes 393248 | tf_op jit(solution)/shard_map/ppermute | solution.py:236
  281.0 67.2 %while.48 = (s32[]{:T(128)}, f32[1024,6,64]{0,2,1:T(8,128)}, f32[1024,6,64]{0,2,1:T(8,128)}, bf16[2,512,6,64]{1,3,2,0:T(8,128)(2,1)}, s32[2]{0:T(128)S(1)}, /*in...) while((s32[]{:T(128)}, f32[1024,6,64]{0,2,1:T(8,128)}, ...), condition=%wide.region_14.15_spmd.clone, body=%wide.region_12.14_spmd.clone.sunk | while | flops 2064906752 | bytes 217293712 | solution.py:89
  284.1 1.8 fusion.154
  286.0 6.3 multiply_reduce_fusion.7
  292.3 5.1 multiply_convert_fusion.4
  297.4 5.4 bitcast_add_fusion.4
  302.7 6.4 fusion.156
  309.1 4.9 bitcast_add_fusion.5
  316.7 1.8 fusion.154
  318.6 6.3 multiply_reduce_fusion.7
  324.9 5.1 multiply_convert_fusion.4
  329.9 5.8 bitcast_add_fusion.4
  335.7 6.3 fusion.156
  342.0 6.0 bitcast_add_fusion.5
  348.2 2.1 copy.51
  350.6 1.6 convert_element_type.126
  352.3 3.5 convolution_convert_fusion.4
  355.9 2.9 fusion.46
  358.8 1.4 fusion.47
  360.2 2.6 pad_maximum_fusion.1
  363.9 2.9 fusion.44
  366.9 1.4 fusion.45
  368.3 2.6 pad_maximum_fusion
  371.5 3.8 fusion.83
  375.2 1.7 copy-done.12
  377.0 1.5 collective-permute-start.3
  378.7 49.9 %psum.7 = f32[9216]{0:T(1024)S(1)} all-reduce(f32[9216]{0:T(1024)S(1)} %constant_dynamic-update-slice_fusion), channel_id=1, replica_groups=mesh['dp'=16,'tensor'=2] {'dp','tensor'}, use_global_device_ids=true, to_apply=%region_25.26 | all-reduce | flops 9216 | bytes 73728 | tf_op jit(solution)/shard_map/psum | solution.py:292
  429.8 2.8 convert_add_fusion
  434.0 1.5 fusion.88
  435.5 103.8 %reduce-scatter.11.cloned.1.call-done = bf16[48,1536]{1,0:T(8,128)(2,1)} async-done(((bf16[1536,1536]{1,0:T(8,128)(2,1)}), bf16[48,1536]{1,0:T(8,128)(2,1)}) %reduce-scatter.11.cloned.1.call-update) | async-done | bytes 147472 | tf_op jit(solution)/shard_map/reduce_scatter | solution.py:268
  539.4 1.6 convert_bitcast_fusion
  541.0 110.8 %reduce-scatter.9.cloned.1.call-done = bf16[48,1536]{1,0:T(8,128)(2,1)} async-done(((bf16[1536,1536]{1,0:T(8,128)(2,1)}), bf16[48,1536]{1,0:T(8,128)(2,1)}) %reduce-scatter.9.cloned.1.call-update) | async-done | bytes 147472 | tf_op jit(solution)/shard_map/reduce_scatter | solution.py:268
  651.8 1.6 convert_element_type.138
  (226 shorter events, 35.8 us)
Async XLA Ops:
  7.2 46.5 %all-gather.5.cloned.1.call-start = ((), (), s32[]{:S(2)}) async-start(), calls=%async_computation.4 | async-start | bytes 1880064 | tf_op jit(solution)/shard_map/all_gather | solution.py:160
  8.7 100.9 %all-gather.7.cloned.1.call-start = ((), (), s32[]{:S(2)}) async-start(), calls=%async_computation.5 | async-start | bytes 1216512 | tf_op jit(solution)/shard_map/all_gather | solution.py:163
  9.5 166.7 %all-gather.9.cloned.1.call-start = ((), (), s32[]{:S(2)}) async-start(), calls=%async_computation.6 | async-start | bytes 4866048 | tf_op jit(solution)/shard_map/all_gather | solution.py:164
  10.2 230.7 %all-gather.11.cloned.1.call-start = ((), (), s32[]{:S(2)}) async-start(), calls=%async_computation.7 | async-start | bytes 4866048 | tf_op jit(solution)/shard_map/all_gather | solution.py:165
  10.3 20.8 %collective-permute-start = (bf16[512,768]{1,0:T(8,128)(2,1)}, bf16[512,768]{1,0:T(8,128)(2,1)S(1)}, u32[]{:S(2)}, u32[]{:S(2)}) collective-permute-start(bf16[512,768]{1,0:T(8,128)(2,1)} %param.23), channel_id=1, source_target_pairs={{0,1},{1,0},{2,3},{3,2},{4,5},{5,4},{6,7},{7,6},{8,9},{9,8},{10,11... | collective-permute-start | bytes 2359304 | tf_op jit(solution)/shard_map/ppermute | solution.py:159
  13.3 419.3 %reduce-scatter.7.cloned.1.call-start = ((), (), s32[]{:S(2)}) async-start(), calls=%async_computation.9 | async-start | bytes 1216512 | tf_op jit(solution)/shard_map/reduce_scatter | solution.py:268
  32.3 21.4 %copy-start.20 = (bf16[512,768]{1,0:T(8,128)(2,1)}, bf16[512,768]{1,0:T(8,128)(2,1)S(1)}, u32[]{:S(2)}) copy-start(bf16[512,768]{1,0:T(8,128)(2,1)S(1)} %get-tuple-element.315) | copy-start | bytes 2359300
  32.3 21.4 %copy-start.22 = (bf16[512,768]{1,0:T(8,128)(2,1)}, bf16[512,768]{1,0:T(8,128)(2,1)S(1)}, u32[]{:S(2)}) copy-start(bf16[512,768]{1,0:T(8,128)(2,1)S(1)} %get-tuple-element.316) | copy-start | bytes 2359300
  63.8 4.5 copy-start.2
  81.3 4.5 copy-start.2
  94.4 4.6 copy-start.27
  95.5 15.9 %copy-start.39 = (f32[768]{0:T(1024)S(1)}, f32[768]{0:T(1024)}, u32[]{:S(2)}) copy-start(f32[768]{0:T(1024)} %param.30) | copy-start | bytes 9220
  97.4 12.2 %collective-permute-start.1 = (bf16[512,384]{1,0:T(8,128)(2,1)}, bf16[512,384]{1,0:T(8,128)(2,1)S(1)}, u32[]{:S(2)}, u32[]{:S(2)}) collective-permute-start(bf16[512,384]{1,0:T(8,128)(2,1)} %copy.53), channel_id=1, source_target_pairs={{0,1},{1,0},{2,3},{3,2},{4,5},{5,4},{6,7},{7,6},{8,9},{9,8},{10,11... | collective-permute-start | bytes 1179656 | tf_op jit(solution)/shard_map/ppermute | solution.py:184
  109.7 1.8 copy-start.13
  111.4 3.1 copy-start.28
  111.5 3.1 copy-start.36
  176.2 5.8 copy-start.16
  176.2 5.8 copy-start.41
  240.9 3.7 copy-start.7
  240.9 4.0 copy-start.42
  240.9 4.0 copy-start.43
  240.9 4.4 copy-start.50
  245.3 2.0 copy-start.11
  245.3 2.0 copy-start.32
  248.7 2.2 copy-start.46
  250.9 3.2 copy-start.18
  250.9 3.2 copy-start.45
  250.9 6.3 slice-start
  254.1 4.6 copy-start.44
  254.1 3.2 slice-start.1
  262.1 3.9 copy-start.8
  262.1 1.8 copy-start.14
  264.6 3.5 copy-start.24
  266.0 11.6 %collective-permute-start.2 = (bf16[512,384]{1,0:T(8,128)(2,1)}, bf16[512,384]{1,0:T(8,128)(2,1)}, u32[]{:S(2)}, u32[]{:S(2)}) collective-permute-start(bf16[512,384]{1,0:T(8,128)(2,1)} %get-tuple-element.345), channel_id=1, source_target_pairs={{0,1},{1,0},{2,3},{3,2},{4,5},{5,4},{6,7},{7,6},{8,9},{9,8},{10,11... | collective-permute-start | bytes 1179656 | tf_op jit(solution)/shard_map/ppermute | solution.py:236
  268.7 8.9 %copy-start.25 = (bf16[512,384]{1,0:T(8,128)(2,1)S(1)}, bf16[512,384]{1,0:T(8,128)(2,1)}, u32[]{:S(2)}) copy-start(bf16[512,384]{1,0:T(8,128)(2,1)} %copy-done.24) | copy-start | bytes 1179652
  268.7 8.9 %copy-start.26 = (bf16[512,384]{1,0:T(8,128)(2,1)S(1)}, bf16[512,384]{1,0:T(8,128)(2,1)}, u32[]{:S(2)}) copy-start(bf16[512,384]{1,0:T(8,128)(2,1)} %get-tuple-element.346) | copy-start | bytes 1179652
  269.9 164.2 %reduce-scatter.5.cloned.1.call-start = ((), (), s32[]{:S(2)}) async-start(), calls=%async_computation.8 | async-start | bytes 1880064 | tf_op jit(solution)/shard_map/reduce_scatter | solution.py:268
  281.4 4.6 copy-start.4
  286.0 6.3 copy-start
  297.4 11.7 %copy-start.1 = (f32[6,512,1024]{2,1,0:T(8,128)S(1)}, f32[6,512,1024]{2,1,0:T(8,128)}, u32[]{:S(2)}) copy-start(f32[6,512,1024]{2,1,0:T(8,128)} %copy-done) | copy-start | bytes 37748740 | tf_op jit(solution)/shard_map/while/body/eval_jaxpr/while
  302.7 6.4 copy-start.10
  309.1 4.9 copy-start.5
  314.0 4.6 copy-start.4
  318.6 6.3 copy-start
  329.9 12.1 %copy-start.1 = (f32[6,512,1024]{2,1,0:T(8,128)S(1)}, f32[6,512,1024]{2,1,0:T(8,128)}, u32[]{:S(2)}) copy-start(f32[6,512,1024]{2,1,0:T(8,128)} %copy-done) | copy-start | bytes 37748740 | tf_op jit(solution)/shard_map/while/body/eval_jaxpr/while
  335.7 6.3 copy-start.10
  342.0 6.1 copy-start.5
  348.2 2.2 copy-start.3
  350.4 1.8 copy-start.23
  352.3 3.5 copy-start.19
  355.8 183.6 %reduce-scatter.11.cloned.1.call-start = ((), (), s32[]{:S(2)}) async-start(), calls=%async_computation.11 | async-start | bytes 4866048 | tf_op jit(solution)/shard_map/reduce_scatter | solution.py:268
  355.8 3.0 copy-start.47
  362.8 289.0 %reduce-scatter.9.cloned.1.call-start = ((), (), s32[]{:S(2)}) async-start(), calls=%async_computation.10 | async-start | bytes 4866048 | tf_op jit(solution)/shard_map/reduce_scatter | solution.py:268
  363.9 3.0 copy-start.49
  371.4 7.1 %copy-start.31 = (f32[768]{0:T(1024)S(1)}, f32[768]{0:T(1024)}, u32[]{:S(2)}) copy-start(f32[768]{0:T(1024)} %get-tuple-element.305) | copy-start | bytes 9220
  371.4 7.1 %copy-start.38 = (f32[768]{0:T(1024)S(1)}, f32[768]{0:T(1024)}, u32[]{:S(2)}) copy-start(f32[768]{0:T(1024)} %get-tuple-element.251) | copy-start | bytes 9220
  371.4 7.1 %copy-start.37 = (f32[768]{0:T(1024)S(1)}, f32[768]{0:T(1024)}, u32[]{:S(2)}) copy-start(f32[768]{0:T(1024)} %get-tuple-element.256) | copy-start | bytes 9220
  371.4 7.1 %copy-start.33 = (f32[768]{0:T(1024)S(1)}, f32[768]{0:T(1024)}, u32[]{:S(2)}) copy-start(f32[768]{0:T(1024)} %get-tuple-element.303) | copy-start | bytes 9220
  371.4 7.1 %copy-start.30 = (f32[768]{0:T(1024)S(1)}, f32[768]{0:T(1024)}, u32[]{:S(2)}) copy-start(f32[768]{0:T(1024)} %get-tuple-element.253) | copy-start | bytes 9220
  371.4 7.1 %copy-start.29 = (f32[768]{0:T(1024)S(1)}, f32[768]{0:T(1024)}, u32[]{:S(2)}) copy-start(f32[768]{0:T(1024)} %get-tuple-element.258) | copy-start | bytes 9220
  371.5 7.2 %copy-start.34 = (f32[1536]{0:T(1024)S(1)}, f32[1536]{0:T(1024)}, u32[]{:S(2)}) copy-start(f32[1536]{0:T(1024)} %get-tuple-element.347) | copy-start | bytes 18436
  371.5 7.2 %copy-start.35 = (f32[1536]{0:T(1024)S(1)}, f32[1536]{0:T(1024)}, u32[]{:S(2)}) copy-start(f32[1536]{0:T(1024)} %get-tuple-element.349) | copy-start | bytes 18436
  376.9 52.9 %copy-start.9 = (f32[512,768]{1,0:T(8,128)S(1)}, f32[512,768]{1,0:T(8,128)}, u32[]{:S(2)}) copy-start(f32[512,768]{1,0:T(8,128)} %copy-done.8) | copy-start | bytes 4718596
  377.0 52.8 %collective-permute-start.3 = (bf16[512,768]{1,0:T(8,128)(2,1)S(1)}, bf16[512,768]{1,0:T(8,128)(2,1)S(1)}, u32[]{:S(2)}, u32[]{:S(2)}) collective-permute-start(bf16[512,768]{1,0:T(8,128)(2,1)S(1)} %dynamic-slice_convert_fusion), channel_id=1, source_target_pairs={{0,1},{1,0},{2,3},{3,2},{4,5},{5,4},{6,7},{7,6},{8,9},{9,8},{10,11... | collective-permute-start | bytes 2359304 | tf_op jit(solution)/shard_map/ppermute | solution.py:258
  (7 other events, 9.5 us)
Sparse Core Ops, SparseCore 0:
  10.7 42.8 all-gather.4
  56.6 53.0 all-gather.6
  112.6 63.5 all-gather.8
  179.0 61.8 all-gather.10
  270.0 95.4 reduce-scatter.6
  369.1 58.4 reduce-scatter.4
  433.0 106.2 reduce-scatter.10
  544.8 106.8 reduce-scatter.8
where the time goes:
time: 665 us; the launch traced here: 660 us
  waiting for transfers between devices  387 us (58%)
  matrix products  123 us (18%)
  blocking collectives  49.9 us (8%)
  other arithmetic  49.1 us (7%)
  local copies, waits for them, and re-layouts  25.9 us (4%)
  between operations  15.1 us (2%)
  starting transfers between devices  7.84 us (1%)
    reduce_scatter x4, waiting for transfers between devices, scatter(): lax.psum_scatter(partial.reshape(-1, partial.shape[-1]), axes, scatter_di...  215 us
    all_gather x1, waiting for transfers between devices, on_device(): full_inner = lax.all_gather(inner_weight, whole, axis=0, tiled=True)  60.4 us
    all_gather x1, waiting for transfers between devices, on_device(): full_outer = lax.all_gather(outer_weight.T, whole, axis=0, tiled=True)  55.4 us
    dot_general x21, matrix products, mix(): lax.dot_general(left, right, (dims, ((), ())), preferred_element_type=jnp...  51.2 us
    psum x1, blocking collectives, on_device(): summed = lax.psum(jnp.concatenate(pieces), ('dp', 'tensor'))  49.9 us
    all_gather x1, waiting for transfers between devices, on_device(): lax.all_gather(jnp.concatenate([query_weight, key_weight, value_weight],...  21.4 us
    ppermute x1, waiting for transfers between devices, on_device(): other_tokens = lax.ppermute(tokens, 'tensor', swap)  16.1 us
    dot_general x2, matrix products, one_block(): jnp.einsum('hqk,khd->qhd', probs_low, value_seq, preferred_element_type=j...  15.6 us
  transfers between devices with their start and end apart: 12, of which 8 were waited for; matrix products, arithmetic and copies ran while one was open for 25% of the time, Pallas kernels for 0%

commit v1 on v0

--- a/solution.py
+++ b/solution.py
@@ -289,7 +289,7 @@
         second_shift_grad,
         inner_bias_grad,
     ]
-    summed = lax.psum(jnp.concatenate(pieces), ("dp", "tensor"))
+    summed = jnp.sum(lax.all_gather(jnp.concatenate(pieces), ("dp", "tensor")), axis=0)
     rows = summed[: 8 * width].reshape(8, width)
     return (
         layer_output,

time: 665 us -> 720 us (1.083)
  waiting for transfers between devices: 387 us -> 492 us
  blocking collectives: 49.9 us -> 0 us
    reduce_scatter x4, waiting for transfers between devices: 215 us -> 280 us  [scatter(): lax.psum_scatter(partial.reshape(-1, partial.shape[-1]), axes, scatter_di...]
    psum x1 -> x0, blocking collectives: 49.9 us -> none  [on_device(): summed = lax.psum(jnp.concatenate(pieces), ('dp', 'tensor'))]
    all_gather x0 -> x1, waiting for transfers between devices: none -> 21.7 us  [on_device(): lax.all_gather(jnp.concatenate(pieces), ('dp', 'tensor'))]
    ppermute x1, waiting for transfers between devices: 0.01 us -> 18.6 us  [on_device(): lax.ppermute(lax.dynamic_slice_in_dim(partial_input, other_start, own_row...]
  transfers between devices with their start and end apart: 12 -> 13, of which waited for: 8 -> 11; matrix products, arithmetic and copies ran while one was open for 25% -> 23% of each run, Pallas kernels for 0% -> 0%
where the time goes in v1:
time: 720 us; the launch traced here: 716 us
  waiting for transfers between devices  492 us (68%)
  matrix products  124 us (17%)
  other arithmetic  47.7 us (7%)
  local copies, waits for them, and re-layouts  26 us (4%)
  between operations  14.9 us (2%)
  starting transfers between devices  8.08 us (1%)
    reduce_scatter x4, waiting for transfers between devices, scatter(): lax.psum_scatter(partial.reshape(-1, partial.shape[-1]), axes, scatter_di...  280 us
    all_gather x1, waiting for transfers between devices, on_device(): full_inner = lax.all_gather(inner_weight, whole, axis=0, tiled=True)  60.4 us
    all_gather x1, waiting for transfers between devices, on_device(): full_outer = lax.all_gather(outer_weight.T, whole, axis=0, tiled=True)  55.4 us
    dot_general x21, matrix products, mix(): lax.dot_general(left, right, (dims, ((), ())), preferred_element_type=jnp...  52.6 us
    all_gather x1, waiting for transfers between devices, on_device(): lax.all_gather(jnp.concatenate(pieces), ('dp', 'tensor'))  21.7 us
    all_gather x1, waiting for transfers between devices, on_device(): lax.all_gather(jnp.concatenate([query_weight, key_weight, value_weight],...  21.4 us
    ppermute x1, waiting for transfers between devices, on_device(): lax.ppermute(lax.dynamic_slice_in_dim(partial_input, other_start, own_row...  18.6 us
    ppermute x1, waiting for transfers between devices, on_device(): other_tokens = lax.ppermute(tokens, 'tensor', swap)  16.1 us
  transfers between devices with their start and end apart: 13, of which 11 were waited for; matrix products, arithmetic and copies ran while one was open for 23% of the time, Pallas kernels for 0%

profile of v1, /device:TPU:0, one launch (start us, length us, event | category | flops | bytes accessed | tf_op | source)
XLA Modules:
  0.0 716.1 jit_solution(15956055230531033520)
XLA Ops:
  7.2 1.5 pad_maximum_fusion.8
  10.3 3.0 collective-permute-start
  14.9 16.1 %collective-permute-done = bf16[512,768]{1,0:T(8,128)(2,1)S(1)} collective-permute-done((bf16[512,768]{1,0:T(8,128)(2,1)}, bf16[512,768]{1,0:T(8,128)(2,1)S(1)}, u32[]{:S(2)}, u32[]{:S(2)}) %collective-permute-start) | collective-permute-done | bytes 786464 | tf_op jit(solution)/shard_map/ppermute | solution.py:159
  32.3 21.4 %all-gather.7.cloned.1.call-done = bf16[768,1152]{1,0:T(8,128)(2,1)} async-done(((bf16[48,1152]{1,0:T(8,128)(2,1)}), bf16[768,1152]{1,0:T(8,128)(2,1)}) %all-gather.7.cloned.1.call-update) | async-done | bytes 1769488 | tf_op jit(solution)/shard_map/all_gather | solution.py:160
  53.7 3.7 add_convert_fusion
  58.6 35.0 %while.47 = (s32[]{:T(128)}, bf16[2,512,6,64]{1,3,2,0:T(8,128)(2,1)S(1)}, f32[2,6,512]{2,1,0:T(8,128)S(1)}, s32[2]{0:T(128)S(1)}, s32[1024]{0:T(1024)S(1)}, /*in...) while((s32[]{:T(128)}, ...), condition=%wide.region_3.4_spmd, body=%wide.region_0.3_spmd.sunk | while | flops 842201600 | bytes 92672224 | solution.py:50
  61.4 2.4 fusion.143
  63.9 3.7 exponential_reduce_fusion.2
  68.4 7.8 %fusion.144 = bf16[2,512,6,64]{1,3,2,0:T(8,128)(2,1)S(1)} fusion(bf16[2,512,6,64]{1,3,2,0:T(8,128)(2,1)S(1)} %get-tuple-element.507, s32[]{:T(128)} %get-tuple-element.506, bf16[1024,6,64]{0,2,1:T(8,128)(2,1)S(1)} %get-tuple-element.527, f32[6,512,1024]{2,1,0:T(8,128)} %copy-done.2, f32[6,512]{1,0:T(8,128)S(1)} %get-tuple-element.477, ...), kind=kOutput, calls=%fused_computation.11.clone.1 | convolution fusion | flops 415432704 | bytes 14303236 | tf_op jit(solution)/shard_map/while/body/eval_jaxpr/while/body/eval_jaxpr/hqk,khd->qhd/dot_general | solution.py:45
  78.8 2.4 fusion.143
  81.3 3.7 exponential_reduce_fusion.2
  85.8 7.8 %fusion.144 = bf16[2,512,6,64]{1,3,2,0:T(8,128)(2,1)S(1)} fusion(bf16[2,512,6,64]{1,3,2,0:T(8,128)(2,1)S(1)} %get-tuple-element.507, s32[]{:T(128)} %get-tuple-element.506, bf16[1024,6,64]{0,2,1:T(8,128)(2,1)S(1)} %get-tuple-element.527, f32[6,512,1024]{2,1,0:T(8,128)} %copy-done.2, f32[6,512]{1,0:T(8,128)S(1)} %get-tuple-element.477, ...), kind=kOutput, calls=%fused_computation.11.clone.1 | convolution fusion | flops 415432704 | bytes 14303236 | tf_op jit(solution)/shard_map/while/body/eval_jaxpr/while/body/eval_jaxpr/hqk,khd->qhd/dot_general | solution.py:45
  95.5 1.9 copy.69
  97.4 1.6 collective-permute-start.1
  100.2 9.4 %all-gather.9.cloned.1.call-done = bf16[1536,384]{1,0:T(8,128)(2,1)} async-done(((bf16[48,384]{1,0:T(8,128)(2,1)}), bf16[1536,384]{1,0:T(8,128)(2,1)}) %all-gather.9.cloned.1.call-update) | async-done | bytes 1179664 | tf_op jit(solution)/shard_map/all_gather | solution.py:163
  109.7 1.8 fusion.77
  111.5 1.9 fusion.92
  115.7 60.4 %all-gather.11.cloned.1.call-done = bf16[1536,1536]{1,0:T(8,128)(2,1)} async-done(((bf16[48,1536]{1,0:T(8,128)(2,1)}), bf16[1536,1536]{1,0:T(8,128)(2,1)}) %all-gather.11.cloned.1.call-update) | async-done | bytes 4718608 | tf_op jit(solution)/shard_map/all_gather | solution.py:164
  176.2 5.8 multiply_convert_fusion.1
  182.0 3.5 multiply_convert_fusion.2
  185.5 55.4 %all-gather.13.cloned.1.call-done = bf16[1536,1536]{1,0:T(8,128)(2,1)} async-done(((bf16[48,1536]{1,0:T(8,128)(2,1)}), bf16[1536,1536]{1,0:T(8,128)(2,1)}) %all-gather.13.cloned.1.call-update) | async-done | bytes 4718608 | tf_op jit(solution)/shard_map/all_gather | solution.py:165
  240.9 3.7 fusion.54
  245.3 1.7 fusion.93
  248.7 2.1 fusion.84
  250.9 3.2 convert_reduce_fusion.2
  254.1 3.2 convert_reduce_fusion.1
  258.7 2.3 multiply_reduce_fusion.1
  262.2 1.8 copy-done.13
  264.6 1.5 broadcast_select_fusion.4
  266.0 1.4 collective-permute-start.2
  269.9 7.7 %collective-permute-done.2 = bf16[512,384]{1,0:T(8,128)(2,1)} collective-permute-done((bf16[512,384]{1,0:T(8,128)(2,1)}, bf16[512,384]{1,0:T(8,128)(2,1)}, u32[]{:S(2)}, u32[]{:S(2)}) %collective-permute-start.2) | collective-permute-done | bytes 393248 | tf_op jit(solution)/shard_map/ppermute | solution.py:236
  281.0 67.2 %while.48 = (s32[]{:T(128)}, f32[1024,6,64]{0,2,1:T(8,128)}, f32[1024,6,64]{0,2,1:T(8,128)}, bf16[2,512,6,64]{1,3,2,0:T(8,128)(2,1)}, s32[2]{0:T(128)S(1)}, /*in...) while((s32[]{:T(128)}, f32[1024,6,64]{0,2,1:T(8,128)}, ...), condition=%wide.region_14.15_spmd.clone, body=%wide.region_12.14_spmd.clone.sunk | while | flops 2064906752 | bytes 217293712 | solution.py:89
  284.1 1.8 fusion.154
  286.0 6.3 multiply_reduce_fusion.7
  292.3 5.0 multiply_convert_fusion.4
  297.3 5.3 bitcast_add_fusion.4
  302.7 6.4 fusion.156
  309.1 4.8 bitcast_add_fusion.5
  316.6 1.8 fusion.154
  318.5 6.3 multiply_reduce_fusion.7
  324.8 5.0 multiply_convert_fusion.4
  329.9 5.7 bitcast_add_fusion.4
  335.6 6.3 fusion.156
  341.9 6.0 bitcast_add_fusion.5
  348.1 2.1 copy.67
  350.6 1.6 convert_element_type.126
  353.5 4.9 convolution_convert_fusion.4
  358.5 2.9 fusion.46
  361.4 1.4 fusion.47
  362.9 2.5 pad_maximum_fusion.1
  366.5 2.9 fusion.44
  370.9 2.6 pad_maximum_fusion
  373.5 3.7 fusion.83
  377.4 1.5 collective-permute-start.3
  378.8 18.6 %collective-permute-done.3 = bf16[512,768]{1,0:T(8,128)(2,1)S(1)} collective-permute-done((bf16[512,768]{1,0:T(8,128)(2,1)S(1)}, bf16[512,768]{1,0:T(8,128)(2,1)S(1)}, u32[]{:S(2)}, u32[]{:S(2)}) %collective-permute-start.3) | collective-permute-done | bytes 786464 | tf_op jit(solution)/shard_map/ppermute | solution.py:258
  397.5 1.4 convert_add_fusion
  400.3 21.7 %all-gather.15.cloned.1.call-done = f32[294912]{0:T(1024)} async-done(((f32[9216]{0:T(1024)}), f32[294912]{0:T(1024)}) %all-gather.15.cloned.1.call-update) | async-done | bytes 1179664 | tf_op jit(solution)/shard_map/all_gather | solution.py:292
  422.0 1.4 reshape.342
  424.8 59.0 %reduce-scatter.5.cloned.1.call-done = bf16[48,1152]{1,0:T(8,128)(2,1)} async-done(((bf16[768,1152]{1,0:T(8,128)(2,1)}), bf16[48,1152]{1,0:T(8,128)(2,1)}) %reduce-scatter.5.cloned.1.call-update) | async-done | bytes 110608 | tf_op jit(solution)/shard_map/reduce_scatter | solution.py:268
  483.8 1.5 fusion.88
  485.3 110.4 %reduce-scatter.11.cloned.1.call-done = bf16[48,1536]{1,0:T(8,128)(2,1)} async-done(((bf16[1536,1536]{1,0:T(8,128)(2,1)}), bf16[48,1536]{1,0:T(8,128)(2,1)}) %reduce-scatter.11.cloned.1.call-update) | async-done | bytes 147472 | tf_op jit(solution)/shard_map/reduce_scatter | solution.py:268
  595.7 1.6 convert_bitcast_fusion
  597.3 110.4 %reduce-scatter.9.cloned.1.call-done = bf16[48,1536]{1,0:T(8,128)(2,1)} async-done(((bf16[1536,1536]{1,0:T(8,128)(2,1)}), bf16[48,1536]{1,0:T(8,128)(2,1)}) %reduce-scatter.9.cloned.1.call-update) | async-done | bytes 147472 | tf_op jit(solution)/shard_map/reduce_scatter | solution.py:268
  707.7 1.6 convert_element_type.138
  (228 shorter events, 39.3 us)
Async XLA Ops:
  7.2 46.5 %all-gather.7.cloned.1.call-start = ((), (), s32[]{:S(2)}) async-start(), calls=%async_computation.4 | async-start | bytes 1880064 | tf_op jit(solution)/shard_map/all_gather | solution.py:160
  8.7 100.9 %all-gather.9.cloned.1.call-start = ((), (), s32[]{:S(2)}) async-start(), calls=%async_computation.5 | async-start | bytes 1216512 | tf_op jit(solution)/shard_map/all_gather | solution.py:163
  9.5 166.7 %all-gather.11.cloned.1.call-start = ((), (), s32[]{:S(2)}) async-start(), calls=%async_computation.6 | async-start | bytes 4866048 | tf_op jit(solution)/shard_map/all_gather | solution.py:164
  10.2 230.7 %all-gather.13.cloned.1.call-start = ((), (), s32[]{:S(2)}) async-start(), calls=%async_computation.7 | async-start | bytes 4866048 | tf_op jit(solution)/shard_map/all_gather | solution.py:165
  10.3 20.8 %collective-permute-start = (bf16[512,768]{1,0:T(8,128)(2,1)}, bf16[512,768]{1,0:T(8,128)(2,1)S(1)}, u32[]{:S(2)}, u32[]{:S(2)}) collective-permute-start(bf16[512,768]{1,0:T(8,128)(2,1)} %param.23), channel_id=1, source_target_pairs={{0,1},{1,0},{2,3},{3,2},{4,5},{5,4},{6,7},{7,6},{8,9},{9,8},{10,11... | collective-permute-start | bytes 2359304 | tf_op jit(solution)/shard_map/ppermute | solution.py:159
  13.3 385.6 %reduce-scatter.7.cloned.1.call-start = ((), (), s32[]{:S(2)}) async-start(), calls=%async_computation.9 | async-start | bytes 1216512 | tf_op jit(solution)/shard_map/reduce_scatter | solution.py:268
  32.3 21.4 %copy-start.19 = (bf16[512,768]{1,0:T(8,128)(2,1)}, bf16[512,768]{1,0:T(8,128)(2,1)S(1)}, u32[]{:S(2)}) copy-start(bf16[512,768]{1,0:T(8,128)(2,1)S(1)} %get-tuple-element.315) | copy-start | bytes 2359300
  32.3 21.4 %copy-start.20 = (bf16[512,768]{1,0:T(8,128)(2,1)}, bf16[512,768]{1,0:T(8,128)(2,1)S(1)}, u32[]{:S(2)}) copy-start(bf16[512,768]{1,0:T(8,128)(2,1)S(1)} %get-tuple-element.316) | copy-start | bytes 2359300
  63.9 4.5 copy-start.2
  81.3 4.5 copy-start.2
  94.4 4.6 copy-start.26
  95.5 15.9 %copy-start.38 = (f32[768]{0:T(1024)S(1)}, f32[768]{0:T(1024)}, u32[]{:S(2)}) copy-start(f32[768]{0:T(1024)} %param.30) | copy-start | bytes 9220
  97.4 12.2 %collective-permute-start.1 = (bf16[512,384]{1,0:T(8,128)(2,1)}, bf16[512,384]{1,0:T(8,128)(2,1)S(1)}, u32[]{:S(2)}, u32[]{:S(2)}) collective-permute-start(bf16[512,384]{1,0:T(8,128)(2,1)} %copy.69), channel_id=1, source_target_pairs={{0,1},{1,0},{2,3},{3,2},{4,5},{5,4},{6,7},{7,6},{8,9},{9,8},{10,11... | collective-permute-start | bytes 1179656 | tf_op jit(solution)/shard_map/ppermute | solution.py:184
  111.4 3.1 copy-start.27
  111.4 3.1 copy-start.35
  176.2 5.8 copy-start.15
  176.2 5.8 copy-start.40
  240.9 3.7 copy-start.7
  240.9 4.0 copy-start.41
  240.9 4.0 copy-start.42
  240.9 4.4 copy-start.49
  245.3 2.0 copy-start.11
  245.3 2.0 copy-start.31
  248.7 2.2 copy-start.45
  250.9 3.2 copy-start.17
  250.9 3.2 copy-start.44
  250.9 6.3 slice-start
  254.1 4.6 copy-start.43
  254.1 3.2 slice-start.1
  262.1 3.9 copy-start.8
  262.1 1.8 copy-start.13
  264.5 3.5 copy-start.21
  266.0 11.6 %collective-permute-start.2 = (bf16[512,384]{1,0:T(8,128)(2,1)}, bf16[512,384]{1,0:T(8,128)(2,1)}, u32[]{:S(2)}, u32[]{:S(2)}) collective-permute-start(bf16[512,384]{1,0:T(8,128)(2,1)} %get-tuple-element.345), channel_id=1, source_target_pairs={{0,1},{1,0},{2,3},{3,2},{4,5},{5,4},{6,7},{7,6},{8,9},{9,8},{10,11... | collective-permute-start | bytes 1179656 | tf_op jit(solution)/shard_map/ppermute | solution.py:236
  268.7 8.9 %copy-start.22 = (bf16[512,384]{1,0:T(8,128)(2,1)S(1)}, bf16[512,384]{1,0:T(8,128)(2,1)}, u32[]{:S(2)}) copy-start(bf16[512,384]{1,0:T(8,128)(2,1)} %copy-done.21) | copy-start | bytes 1179652
  268.7 8.9 %copy-start.23 = (bf16[512,384]{1,0:T(8,128)(2,1)S(1)}, bf16[512,384]{1,0:T(8,128)(2,1)}, u32[]{:S(2)}) copy-start(bf16[512,384]{1,0:T(8,128)(2,1)} %get-tuple-element.346) | copy-start | bytes 1179652
  269.9 152.1 %all-gather.15.cloned.1.call-start = ((), (), s32[]{:S(2)}) async-start(), calls=%async_computation.12 | async-start | bytes 1216512 | tf_op jit(solution)/shard_map/all_gather | solution.py:292
  281.3 4.6 copy-start.4
  286.0 6.3 copy-start
  297.3 11.7 %copy-start.1 = (f32[6,512,1024]{2,1,0:T(8,128)S(1)}, f32[6,512,1024]{2,1,0:T(8,128)}, u32[]{:S(2)}) copy-start(f32[6,512,1024]{2,1,0:T(8,128)} %copy-done) | copy-start | bytes 37748740 | tf_op jit(solution)/shard_map/while/body/eval_jaxpr/while
  302.7 6.4 copy-start.10
  309.1 4.8 copy-start.5
  313.9 4.6 copy-start.4
  318.5 6.3 copy-start
  329.9 12.1 %copy-start.1 = (f32[6,512,1024]{2,1,0:T(8,128)S(1)}, f32[6,512,1024]{2,1,0:T(8,128)}, u32[]{:S(2)}) copy-start(f32[6,512,1024]{2,1,0:T(8,128)} %copy-done) | copy-start | bytes 37748740 | tf_op jit(solution)/shard_map/while/body/eval_jaxpr/while
  335.6 6.3 copy-start.10
  341.9 6.0 copy-start.5
  348.1 2.2 copy-start.3
  350.4 2.1 copy-start.24
  350.5 2.1 copy-start.30
  350.5 2.2 copy-start.37
  350.5 2.2 copy-start.36
  350.5 2.2 copy-start.32
  350.5 2.2 copy-start.29
  350.5 2.2 copy-start.28
  350.5 2.2 copy-start.33
  350.5 2.2 copy-start.34
  353.4 5.0 copy-start.18
  353.4 130.3 %reduce-scatter.5.cloned.1.call-start = ((), (), s32[]{:S(2)}) async-start(), calls=%async_computation.8 | async-start | bytes 1880064 | tf_op jit(solution)/shard_map/reduce_scatter | solution.py:268
  358.4 237.3 %reduce-scatter.11.cloned.1.call-start = ((), (), s32[]{:S(2)}) async-start(), calls=%async_computation.11 | async-start | bytes 4866048 | tf_op jit(solution)/shard_map/reduce_scatter | solution.py:268
  358.5 3.0 copy-start.46
  365.4 342.3 %reduce-scatter.9.cloned.1.call-start = ((), (), s32[]{:S(2)}) async-start(), calls=%async_computation.10 | async-start | bytes 4866048 | tf_op jit(solution)/shard_map/reduce_scatter | solution.py:268
  366.5 2.9 copy-start.48
  377.3 20.2 %copy-start.9 = (f32[512,768]{1,0:T(8,128)S(1)}, f32[512,768]{1,0:T(8,128)}, u32[]{:S(2)}) copy-start(f32[512,768]{1,0:T(8,128)} %copy-done.8) | copy-start | bytes 4718596
  377.4 20.1 %collective-permute-start.3 = (bf16[512,768]{1,0:T(8,128)(2,1)S(1)}, bf16[512,768]{1,0:T(8,128)(2,1)S(1)}, u32[]{:S(2)}, u32[]{:S(2)}) collective-permute-start(bf16[512,768]{1,0:T(8,128)(2,1)S(1)} %dynamic-slice_convert_fusion), channel_id=1, source_target_pairs={{0,1},{1,0},{2,3},{3,2},{4,5},{5,4},{6,7},{7,6},{8,9},{9,8},{10,11... | collective-permute-start | bytes 2359304 | tf_op jit(solution)/shard_map/ppermute | solution.py:258
  (7 other events, 8.5 us)
Sparse Core Ops, SparseCore 0:
  10.7 42.8 all-gather.6
  56.6 53.0 all-gather.8
  112.6 63.5 all-gather.10
  179.0 61.8 all-gather.12
  270.0 95.3 reduce-scatter.6
  368.8 53.1 all-gather.14
  425.8 57.9 reduce-scatter.4
  489.2 106.4 reduce-scatter.10
  601.2 106.4 reduce-scatter.8
